TPU v7x, 256 devices: a whole 4x4x8 slice. The times are simulated.
256 devices in a mesh: grp: 8 (over x, core), vocab: 32 (over y, z).
Axes of the slice: x: 4, y: 4, z: 8, core: 2. Of those that a mesh axis runs over, the one named last changes fastest.
Arguments:
- hidden: bfloat16 [1024, 16384], P('grp', 'vocab'), may hold values from -6 to 6
- flags: int32 [1024, 1], P('grp'), may hold values from 0 to 8; in each aligned block of 128 rows (0 to 127, 128 to 255, ...) at most 16 rows name the same one
- targets: int32 [1024], P('grp'), may hold values from 0 to 65535
- head: bfloat16 [16384, 65536], P('grp', 'vocab'), may hold values from -0.140625 to 0.140625
- lengths: int32 [8, 8], P('grp'), may hold values from 1 to 64, 128 in all within a row
Outputs:
- token_scores: float32 [1024], P('grp')
- doc_scores: float32 [8, 8], P('grp')
Inputs may be any that keep to these rules, and one draw needn't show every extreme that they name: `flags`: A value below 8 names the scorer group of a scored row. Within the 128 rows of one shard no value occurs more than 16 times, and in every draw some value occurs exactly 16 times in some shard.
All inputs are finite; a program needn't handle non-finite values.
Results may differ from a plain program's by a relative error of at most 0.0003.
Values may be sent and summed in bfloat16 or wider, within the bound.
A program may use at most 128 MiB of HBM per device.

v0:
```python
import jax
import jax.numpy as jnp
from jax import lax
from jax.sharding import PartitionSpec as P


def combined_all(part, axis, combine):
    gathered = jax.tree.map(lambda a: lax.all_gather(a, axis), part)

    def take(source):
        return jax.tree.map(lambda a: lax.dynamic_index_in_dim(a, source, 0, False), gathered)

    return lax.fori_loop(
        1, lax.axis_size(axis), lambda source, state: combine(state, take(source)), take(0)
    )


def slot_table(flag_col, groups, capacity, shard_rows):
    values = jnp.arange(groups + 1, dtype=jnp.int32)
    onehot = (flag_col[:, None] == values[None, :]).astype(jnp.int32)
    ranking = jnp.sum((jnp.cumsum(onehot, axis=0) - 1) * onehot, axis=1)
    where_to = jnp.where(flag_col < groups, flag_col * capacity + ranking, groups * capacity)
    table = jnp.full((groups * capacity + 1,), -1, jnp.int32)
    table = table.at[where_to].set(jnp.arange(shard_rows, dtype=jnp.int32))
    return table[: groups * capacity]


def combine_stats(left, right):
    row_max = jnp.maximum(left[0], right[0])
    left_gap = left[0] - row_max
    right_gap = right[0] - row_max
    left_fac = jnp.exp(left_gap)
    right_fac = jnp.exp(right_gap)
    row_total = left_fac * left[1] + right_fac * right[1]
    first_mom = left_fac * (left[2] + left_gap * left[1]) + right_fac * (
        right[2] + right_gap * right[1]
    )
    second_mom = left_fac * (left[3] + 2.0 * left_gap * left[2] + left_gap * left_gap * left[1])
    second_mom = second_mom + right_fac * (
        right[3] + 2.0 * right_gap * right[2] + right_gap * right_gap * right[1]
    )
    return (row_max, row_total, first_mom, second_mom)


def local_stats(logits, target_ids, columns, axis):
    row_max = jnp.max(logits, axis=axis)
    shifted = logits - jnp.expand_dims(row_max, axis)
    scaled = jnp.exp(shifted)
    row_total = jnp.sum(scaled, axis=axis)
    first_mom = jnp.sum(scaled * shifted, axis=axis)
    second_mom = jnp.sum(scaled * shifted * shifted, axis=axis)
    is_target = target_ids[:, None] == columns[None, :]
    target_val = jnp.sum(jnp.where(is_target, logits, jnp.float32(0.0)), axis=axis)
    return (row_max, row_total, first_mom, second_mom, target_val)


def final_scores(target_ids, row_max, row_total, first_mom, second_mom, target_val):
    mean_shift = first_mom / row_total
    row_var = second_mom / row_total - mean_shift * mean_shift
    return jnp.where(
        target_ids >= 0,
        (target_val - row_max - mean_shift) / jnp.sqrt(jnp.maximum(row_var, 1.0)),
        jnp.float32(0.0),
    )


def shards(hidden, flags, targets, head, lengths):
    groups = lax.axis_size("grp")
    shard_rows = hidden.shape[0]
    capacity = shard_rows // groups
    vocab_dev = head.shape[1]
    my_vocab = lax.axis_index("vocab")
    flag_col = flags[:, 0]
    table = slot_table(flag_col, groups, capacity, shard_rows)
    is_live = table >= 0
    safe_rows = jnp.maximum(table, 0)
    pieces = jnp.where(is_live[:, None], hidden[safe_rows], jnp.zeros((), jnp.bfloat16))
    slot_targets = jnp.where(is_live, targets[safe_rows], -1)
    arrived = lax.all_to_all(
        pieces.reshape(groups, capacity, pieces.shape[1]),
        "grp",
        split_axis=0,
        concat_axis=0,
        tiled=True,
    )
    full_rows = lax.all_gather(
        arrived.reshape(shard_rows, pieces.shape[1]), "vocab", axis=1, tiled=True
    )
    block_rows = lax.all_to_all(full_rows, "grp", split_axis=1, concat_axis=0, tiled=True)
    target_ids = lax.all_to_all(
        slot_targets.reshape(groups, capacity), "grp", split_axis=0, concat_axis=0, tiled=True
    ).reshape(shard_rows)
    logits = lax.psum_scatter(
        jnp.dot(block_rows, head, preferred_element_type=jnp.float32),
        "grp",
        scatter_dimension=0,
        tiled=True,
    )
    columns = my_vocab * vocab_dev + jnp.arange(vocab_dev, dtype=jnp.int32)
    row_max, row_total, first_mom, second_mom, target_val = local_stats(
        logits, target_ids, columns, 1
    )
    row_max, row_total, first_mom, second_mom = combined_all(
        (row_max, row_total, first_mom, second_mom), "vocab", combine_stats
    )
    target_val = lax.psum(target_val, "vocab")
    token_scores = final_scores(target_ids, row_max, row_total, first_mom, second_mom, target_val)
    returned = lax.all_to_all(
        token_scores.reshape(groups, capacity), "grp", split_axis=0, concat_axis=0, tiled=True
    ).reshape(shard_rows)
    row_val = (
        jnp.zeros((shard_rows + 1,), jnp.float32)
        .at[jnp.where(is_live, table, shard_rows)]
        .set(returned)[:shard_rows]
    )
    flagged = (flag_col < groups).astype(jnp.float32)
    doc_ends = jnp.cumsum(lengths[0])
    doc_starts = doc_ends - lengths[0]
    positions = jnp.arange(shard_rows, dtype=jnp.int32)
    membership = (
        (positions[None, :] >= doc_starts[:, None]) & (positions[None, :] < doc_ends[:, None])
    ).astype(jnp.float32)
    sums = jnp.sum(membership * row_val[None, :], axis=1)
    counts = jnp.sum(membership * flagged[None, :], axis=1)
    doc_means = (sums / jnp.maximum(counts, 1.0))[None, :]
    return (token_scores, doc_means)


def solution(mesh):
    placed = (P("grp", "vocab"), P("grp", None), P("grp"), P("grp", "vocab"), P("grp", None))
    return jax.shard_map(
        shards, mesh=mesh, in_specs=placed, out_specs=(P("grp"), P("grp", None)), check_vma=False
    )
```

profile of v0, /device:TPU:1, one launch (start us, length us, event | category | flops | bytes accessed | tf_op | source)
XLA Modules:
  0.0 488.9 jit_solution(7191298796290074408)
XLA Ops:
  8.2 0.8 select_reduce_fusion.1
  9.7 1.0 scatter_custom_fusion
  10.8 0.9 gather_fusion.1
  11.7 11.6 %all_to_all.39 = bf16[8,16,512]{2,1,0:T(8,128)(2,1)} all-to-all(bf16[8,16,512]{2,1,0:T(8,128)(2,1)S(1)} %broadcast_select_fusion), channel_id=1, replica_groups=mesh['grp'=8,'vocab'=32] {'grp'}, dimensions={0} | all-to-all | bytes 262144 | tf_op jit(solution)/shard_map/all_to_all | solution.py:79
  23.4 80.8 %all-gather.10.cloned.1.call-done = bf16[128,16384]{1,0:T(8,128)(2,1)} async-done(((bf16[128,512]{1,0:T(8,128)(2,1)}), bf16[128,16384]{1,0:T(8,128)(2,1)}) %all-gather.10.cloned.1.call-update) | async-done | bytes 4194320 | tf_op jit(solution)/shard_map/all_gather | solution.py:86
  104.2 6.4 %copy.16 = bf16[128,16384]{0,1:T(8,128)(2,1)} copy(bf16[128,16384]{1,0:T(8,128)(2,1)} %all-gather.10.cloned.1.call-done) | data formatting | bytes 8388608 | tf_op jit(solution)/shard_map/all_gather | solution.py:86
  110.6 57.6 %all_to_all.40 = bf16[128,8,2048]{0,2,1:T(8,128)(2,1)} all-to-all(bf16[128,8,2048]{0,2,1:T(8,128)(2,1)} %bitcast.91), channel_id=1, replica_groups=mesh['grp'=8,'vocab'=32] {'grp'}, dimensions={1} | all-to-all | bytes 8388608 | tf_op jit(solution)/shard_map/all_to_all | solution.py:89
  168.2 6.5 %copy.17 = bf16[8,128,2048]{2,1,0:T(8,128)(2,1)} copy(bf16[8,128,2048]{1,2,0:T(8,128)(2,1)} %bitcast.92) | data formatting | bytes 8388608 | tf_op jit(solution)/shard_map/all_to_all | solution.py:89
  174.6 14.4 %fusion.21 = f32[1024,2048]{1,0:T(8,128)} fusion(bf16[1024,2048]{1,0:T(8,128)(2,1)} %bitcast.93, bf16[2048,2048]{1,0:T(8,128)(2,1)} %param.10), kind=kOutput, calls=%fused_computation.58 | convolution fusion | flops 8589934592 | bytes 20971520 | tf_op jit(solution)/shard_map/dot_general | solution.py:94
  189.7 1.2 gather_fusion
  191.6 4.2 all-to-all-start
  196.1 4.4 all-to-all-done
  201.7 40.7 %reduce-scatter.2.cloned.1.call-done = f32[128,2048]{1,0:T(8,128)} async-done(((f32[1024,2048]{1,0:T(8,128)}), f32[128,2048]{1,0:T(8,128)}) %reduce-scatter.2.cloned.1.call-update) | async-done | bytes 1048592 | tf_op jit(solution)/shard_map/reduce_scatter | solution.py:93
  242.4 1.4 reduce_max.9
  243.8 31.7 %all-gather.4 = f32[32,1,128]{2,1,0:T(1,128)S(1)} all-gather(f32[1,1,128]{2,1,0:T(1,128)S(1)} %bitcast.100), channel_id=2, replica_groups=mesh['grp'=8,'vocab'=32] {'vocab'}, dimensions={0}, use_global_device_ids=true | all-gather | bytes 16896 | tf_op jit(solution)/shard_map/all_gather | solution.py:8
  275.4 1.7 fusion.11
  277.2 27.1 %all-gather.5 = f32[32,1,128]{2,1,0:T(1,128)S(1)} all-gather(f32[1,1,128]{2,1,0:T(1,128)S(1)} %bitcast.103), channel_id=3, replica_groups=mesh['grp'=8,'vocab'=32] {'vocab'}, dimensions={0}, use_global_device_ids=true | all-gather | bytes 16896 | tf_op jit(solution)/shard_map/all_gather | solution.py:8
  304.3 28.7 %all-gather.6 = f32[32,1,128]{2,1,0:T(1,128)S(1)} all-gather(f32[1,1,128]{2,1,0:T(1,128)S(1)} %bitcast.102), channel_id=4, replica_groups=mesh['grp'=8,'vocab'=32] {'vocab'}, dimensions={0}, use_global_device_ids=true | all-gather | bytes 16896 | tf_op jit(solution)/shard_map/all_gather | solution.py:8
  333.0 27.2 %all-gather.7 = f32[32,1,128]{2,1,0:T(1,128)S(1)} all-gather(f32[1,1,128]{2,1,0:T(1,128)S(1)} %bitcast.101), channel_id=5, replica_groups=mesh['grp'=8,'vocab'=32] {'vocab'}, dimensions={0}, use_global_device_ids=true | all-gather | bytes 16896 | tf_op jit(solution)/shard_map/all_gather | solution.py:8
  360.2 2.7 while.21
  362.9 56.7 %psum.7 = f32[128]{0:T(128)S(1)} all-reduce(f32[128]{0:T(128)S(1)} %get-tuple-element.232), channel_id=1, replica_groups=mesh['grp'=8,'vocab'=32] {'vocab'}, use_global_device_ids=true, to_apply=%region_5.6 | all-reduce | flops 128 | bytes 1024 | tf_op jit(solution)/shard_map/psum | solution.py:106
  420.3 54.2 %all-to-all-start.3 = ((f32[8,1,16]{2,1,0:T(1,128)}), f32[8,1,16]{2,1,0:T(1,128)S(1)}, u32[]{:S(2)}, u32[]{:S(2)}) async-start(f32[8,1,16]{2,1,0:T(1,128)} %bitcast.28), calls=%async_computation.4 | async-start | bytes 8192 | tf_op jit(solution)/shard_map/all_to_all | solution.py:108
  474.5 4.6 all-to-all-done.3
  480.3 1.0 scatter_custom_fusion.1
  (137 shorter events, 9.1 us)
Async XLA Ops:
  7.2 3.6 copy-start
  7.2 97.0 %all-gather.10.cloned.1.call-start = ((), (), s32[]{:S(2)}) async-start(), calls=%async_computation.5 | async-start | bytes 4325376 | tf_op jit(solution)/shard_map/all_gather | solution.py:86
  23.3 219.1 %reduce-scatter.2.cloned.1.call-start = ((), (), s32[]{:S(2)}) async-start(), calls=%async_computation.6 | async-start | bytes 9437184 | tf_op jit(solution)/shard_map/reduce_scatter | solution.py:93
  189.1 0.7 copy-start.1
  189.1 6.8 %copy-start.4 = (s32[1,8]{1,0:T(1,128)S(1)}, s32[1,8]{1,0:T(1,128)}, u32[]{:S(2)}) copy-start(s32[1,8]{1,0:T(1,128)} %param.11) | copy-start | bytes 100
  189.1 285.4 %copy-start.2 = (s32[128,1]{0,1:T(1,128)S(1)}, s32[128,1]{0,1:T(1,128)}, u32[]{:S(2)}) copy-start(s32[128,1]{0,1:T(1,128)} %param.8) | copy-start | bytes 1540
  191.6 8.8 %all-to-all-start = ((s32[8,1,16]{2,1,0:T(1,128)}), s32[8,1,16]{2,1,0:T(1,128)S(1)}, u32[]{:S(2)}, u32[]{:S(2)}) async-start(s32[8,1,16]{2,1,0:T(1,128)} %bitcast.7), calls=%async_computation | async-start | bytes 8192 | tf_op jit(solution)/shard_map/all_to_all | solution.py:90
  419.6 62.5 %copy-start.3 = (f32[128]{0:T(128)}, f32[128]{0:T(128)S(1)}, u32[]{:S(2)}) copy-start(f32[128]{0:T(128)S(1)} %compare_select_fusion.2) | copy-start | bytes 1540
  420.3 58.8 %all-to-all-start.3 = ((f32[8,1,16]{2,1,0:T(1,128)}), f32[8,1,16]{2,1,0:T(1,128)S(1)}, u32[]{:S(2)}, u32[]{:S(2)}) async-start(f32[8,1,16]{2,1,0:T(1,128)} %bitcast.28), calls=%async_computation.4 | async-start | bytes 8192 | tf_op jit(solution)/shard_map/all_to_all | solution.py:108
Sparse Core Ops, SparseCore 0:
  23.4 80.6 all-gather.9
  189.2 53.1 reduce-scatter.1
where the time goes:
time: 490 us; the launch traced here: 489 us
  blocking collectives  241 us (49%)
  waiting for transfers between devices  131 us (27%)
  starting transfers between devices  58.5 us (12%)
  local copies, waits for them, and re-layouts  20.2 us (4%)
  matrix products  14.4 us (3%)
  between operations  14.2 us (3%)
  other arithmetic  9.6 us (2%)
    all_gather x4, blocking collectives, combined_all(): gathered = jax.tree.map(lambda a: lax.all_gather(a, axis), part)  115 us
    all_gather x1, waiting for transfers between devices, shards(): lax.all_gather(arrived.reshape(shard_rows, pieces.shape[1]), 'vocab', axi...  80.8 us
    all_to_all x1, blocking collectives, shards(): lax.all_to_all(full_rows, 'grp', split_axis=1, concat_axis=0, tiled=True)  57.6 us
    psum x1, blocking collectives, shards(): target_val = lax.psum(target_val, 'vocab')  56.7 us
    all_to_all x1, starting transfers between devices, shards(): lax.all_to_all(token_scores.reshape(groups, capacity), 'grp', split_axis=...  54.2 us
    reduce_scatter x1, waiting for transfers between devices, shards(): lax.psum_scatter(jnp.dot(block_rows, head, preferred_element_type=jnp.flo...  40.7 us
    dot_general x1, matrix products, shards(): jnp.dot(block_rows, head, preferred_element_type=jnp.float32)  14.4 us
    all_to_all x1, blocking collectives, shards(): lax.all_to_all(pieces.reshape(groups, capacity, pieces.shape[1]), 'grp',...  11.6 us
  transfers between devices with their start and end apart: 4, of which 4 were waited for; matrix products, arithmetic and copies ran while one was open for 1% of the time, Pallas kernels for 0%

commit v1 on v0

--- a/solution.py
+++ b/solution.py
@@ -2,6 +2,12 @@
 import jax.numpy as jnp
 from jax import lax
 from jax.sharding import PartitionSpec as P
+
+
+def gather_and_add(x, mesh_axis):
+    parts = lax.all_gather(x, mesh_axis, axis=0, tiled=False)
+    total = parts.sum(axis=0)
+    return total
 
 
 def combined_all(part, axis, combine):
@@ -103,7 +109,7 @@
     row_max, row_total, first_mom, second_mom = combined_all(
         (row_max, row_total, first_mom, second_mom), "vocab", combine_stats
     )
-    target_val = lax.psum(target_val, "vocab")
+    target_val = gather_and_add(target_val, "vocab")
     token_scores = final_scores(target_ids, row_max, row_total, first_mom, second_mom, target_val)
     returned = lax.all_to_all(
         token_scores.reshape(groups, capacity), "grp", split_axis=0, concat_axis=0, tiled=True

time: 490 us -> 455 us (0.929)
  blocking collectives: 241 us -> 212 us
  starting transfers between devices: 58.5 us -> 52.2 us
    psum x1 -> x0, blocking collectives: 56.7 us -> none  [shards(): target_val = lax.psum(target_val, 'vocab')]
    all_gather x0 -> x1, blocking collectives: none -> 28.2 us  [gather_and_add(): parts = lax.all_gather(x, mesh_axis, axis=0, tiled=False)]
    all_to_all x1, starting transfers between devices: 54.2 us -> 47.9 us  [shards(): lax.all_to_all(token_scores.reshape(groups, capacity), 'grp', split_axis=...]
where the time goes in v1:
time: 455 us; the launch traced here: 454 us
  blocking collectives  212 us (47%)
  waiting for transfers between devices  131 us (29%)
  starting transfers between devices  52.2 us (11%)
  local copies, waits for them, and re-layouts  20.2 us (4%)
  matrix products  14.4 us (3%)
  between operations  14.2 us (3%)
  other arithmetic  9.64 us (2%)
    all_gather x4, blocking collectives, combined_all(): gathered = jax.tree.map(lambda a: lax.all_gather(a, axis), part)  115 us
    all_gather x1, waiting for transfers between devices, shards(): lax.all_gather(arrived.reshape(shard_rows, pieces.shape[1]), 'vocab', axi...  80.8 us
    all_to_all x1, blocking collectives, shards(): lax.all_to_all(full_rows, 'grp', split_axis=1, concat_axis=0, tiled=True)  57.6 us
    all_to_all x1, starting transfers between devices, shards(): lax.all_to_all(token_scores.reshape(groups, capacity), 'grp', split_axis=...  47.9 us
    reduce_scatter x1, waiting for transfers between devices, shards(): lax.psum_scatter(jnp.dot(block_rows, head, preferred_element_type=jnp.flo...  40.7 us
    all_gather x1, blocking collectives, gather_and_add(): parts = lax.all_gather(x, mesh_axis, axis=0, tiled=False)  28.2 us
    dot_general x1, matrix products, shards(): jnp.dot(block_rows, head, preferred_element_type=jnp.float32)  14.4 us
    all_to_all x1, blocking collectives, shards(): lax.all_to_all(pieces.reshape(groups, capacity, pieces.shape[1]), 'grp',...  11.6 us
  transfers between devices with their start and end apart: 4, of which 4 were waited for; matrix products, arithmetic and copies ran while one was open for 1% of the time, Pallas kernels for 0%

profile of v1, /device:TPU:1, one launch (start us, length us, event | category | flops | bytes accessed | tf_op | source)
XLA Modules:
  0.0 454.2 jit_solution(16105672444419484942)
XLA Ops:
  8.2 0.8 select_reduce_fusion.1
  9.7 1.0 scatter_custom_fusion
  10.8 0.9 gather_fusion.1
  11.7 11.6 %all_to_all.39 = bf16[8,16,512]{2,1,0:T(8,128)(2,1)} all-to-all(bf16[8,16,512]{2,1,0:T(8,128)(2,1)S(1)} %broadcast_select_fusion), channel_id=1, replica_groups=mesh['grp'=8,'vocab'=32] {'grp'}, dimensions={0} | all-to-all | bytes 262144 | tf_op jit(solution)/shard_map/all_to_all | solution.py:85
  23.4 80.8 %all-gather.12.cloned.1.call-done = bf16[128,16384]{1,0:T(8,128)(2,1)} async-done(((bf16[128,512]{1,0:T(8,128)(2,1)}), bf16[128,16384]{1,0:T(8,128)(2,1)}) %all-gather.12.cloned.1.call-update) | async-done | bytes 4194320 | tf_op jit(solution)/shard_map/all_gather | solution.py:92
  104.2 6.4 %copy.16 = bf16[128,16384]{0,1:T(8,128)(2,1)} copy(bf16[128,16384]{1,0:T(8,128)(2,1)} %all-gather.12.cloned.1.call-done) | data formatting | bytes 8388608 | tf_op jit(solution)/shard_map/all_gather | solution.py:92
  110.6 57.6 %all_to_all.40 = bf16[128,8,2048]{0,2,1:T(8,128)(2,1)} all-to-all(bf16[128,8,2048]{0,2,1:T(8,128)(2,1)} %bitcast.92), channel_id=1, replica_groups=mesh['grp'=8,'vocab'=32] {'grp'}, dimensions={1} | all-to-all | bytes 8388608 | tf_op jit(solution)/shard_map/all_to_all | solution.py:95
  168.2 6.5 %copy.17 = bf16[8,128,2048]{2,1,0:T(8,128)(2,1)} copy(bf16[8,128,2048]{1,2,0:T(8,128)(2,1)} %bitcast.93) | data formatting | bytes 8388608 | tf_op jit(solution)/shard_map/all_to_all | solution.py:95
  174.6 14.4 %fusion.21 = f32[1024,2048]{1,0:T(8,128)} fusion(bf16[1024,2048]{1,0:T(8,128)(2,1)} %bitcast.94, bf16[2048,2048]{1,0:T(8,128)(2,1)} %param.10), kind=kOutput, calls=%fused_computation.58 | convolution fusion | flops 8589934592 | bytes 20971520 | tf_op jit(solution)/shard_map/dot_general | solution.py:100
  189.7 1.2 gather_fusion
  191.6 4.2 all-to-all-start
  196.1 4.4 all-to-all-done
  201.7 40.7 %reduce-scatter.2.cloned.1.call-done = f32[128,2048]{1,0:T(8,128)} async-done(((f32[1024,2048]{1,0:T(8,128)}), f32[128,2048]{1,0:T(8,128)}) %reduce-scatter.2.cloned.1.call-update) | async-done | bytes 1048592 | tf_op jit(solution)/shard_map/reduce_scatter | solution.py:99
  242.4 1.4 reduce_max.9
  243.8 31.7 %all-gather.6 = f32[32,1,128]{2,1,0:T(1,128)S(1)} all-gather(f32[1,1,128]{2,1,0:T(1,128)S(1)} %bitcast.101), channel_id=3, replica_groups=mesh['grp'=8,'vocab'=32] {'vocab'}, dimensions={0}, use_global_device_ids=true | all-gather | bytes 16896 | tf_op jit(solution)/shard_map/all_gather | solution.py:14
  275.4 1.7 fusion.11
  277.2 27.1 %all-gather.7 = f32[32,1,128]{2,1,0:T(1,128)S(1)} all-gather(f32[1,1,128]{2,1,0:T(1,128)S(1)} %bitcast.105), channel_id=4, replica_groups=mesh['grp'=8,'vocab'=32] {'vocab'}, dimensions={0}, use_global_device_ids=true | all-gather | bytes 16896 | tf_op jit(solution)/shard_map/all_gather | solution.py:14
  304.3 28.7 %all-gather.8 = f32[32,1,128]{2,1,0:T(1,128)S(1)} all-gather(f32[1,1,128]{2,1,0:T(1,128)S(1)} %bitcast.104), channel_id=5, replica_groups=mesh['grp'=8,'vocab'=32] {'vocab'}, dimensions={0}, use_global_device_ids=true | all-gather | bytes 16896 | tf_op jit(solution)/shard_map/all_gather | solution.py:14
  333.0 27.2 %all-gather.9 = f32[32,1,128]{2,1,0:T(1,128)S(1)} all-gather(f32[1,1,128]{2,1,0:T(1,128)S(1)} %bitcast.103), channel_id=6, replica_groups=mesh['grp'=8,'vocab'=32] {'vocab'}, dimensions={0}, use_global_device_ids=true | all-gather | bytes 16896 | tf_op jit(solution)/shard_map/all_gather | solution.py:14
  360.2 2.7 while.21
  362.9 28.2 %all-gather.5 = f32[32,1,128]{2,1,0:T(1,128)S(1)} all-gather(f32[1,1,128]{2,1,0:T(1,128)S(1)} %bitcast.102), channel_id=2, replica_groups=mesh['grp'=8,'vocab'=32] {'vocab'}, dimensions={0}, use_global_device_ids=true | all-gather | bytes 16896 | tf_op jit(solution)/shard_map/all_gather | solution.py:8
  391.9 47.9 %all-to-all-start.3 = ((f32[8,1,16]{2,1,0:T(1,128)}), f32[8,1,16]{2,1,0:T(1,128)S(1)}, u32[]{:S(2)}, u32[]{:S(2)}) async-start(f32[8,1,16]{2,1,0:T(1,128)} %bitcast.29), calls=%async_computation.4 | async-start | bytes 8192 | tf_op jit(solution)/shard_map/all_to_all | solution.py:114
  439.8 4.6 %all-to-all-done.3 = f32[8,1,16]{2,1,0:T(1,128)S(1)} async-done(((f32[8,1,16]{2,1,0:T(1,128)}), f32[8,1,16]{2,1,0:T(1,128)S(1)}, u32[]{:S(2)}, u32[]{:S(2)}) %all-to-all-start.3) | async-done | bytes 544 | tf_op jit(solution)/shard_map/all_to_all | solution.py:114
  445.6 1.0 scatter_custom_fusion.1
  (138 shorter events, 9.2 us)
Async XLA Ops:
  7.2 3.6 copy-start
  7.2 97.0 %all-gather.12.cloned.1.call-start = ((), (), s32[]{:S(2)}) async-start(), calls=%async_computation.5 | async-start | bytes 4325376 | tf_op jit(solution)/shard_map/all_gather | solution.py:92
  23.3 219.1 %reduce-scatter.2.cloned.1.call-start = ((), (), s32[]{:S(2)}) async-start(), calls=%async_computation.6 | async-start | bytes 9437184 | tf_op jit(solution)/shard_map/reduce_scatter | solution.py:99
  189.1 0.7 copy-start.1
  189.1 6.8 %copy-start.4 = (s32[1,8]{1,0:T(1,128)S(1)}, s32[1,8]{1,0:T(1,128)}, u32[]{:S(2)}) copy-start(s32[1,8]{1,0:T(1,128)} %param.11) | copy-start | bytes 100
  189.1 250.7 %copy-start.2 = (s32[128,1]{0,1:T(1,128)S(1)}, s32[128,1]{0,1:T(1,128)}, u32[]{:S(2)}) copy-start(s32[128,1]{0,1:T(1,128)} %param.8) | copy-start | bytes 1540
  191.6 8.8 %all-to-all-start = ((s32[8,1,16]{2,1,0:T(1,128)}), s32[8,1,16]{2,1,0:T(1,128)S(1)}, u32[]{:S(2)}, u32[]{:S(2)}) async-start(s32[8,1,16]{2,1,0:T(1,128)} %bitcast.7), calls=%async_computation | async-start | bytes 8192 | tf_op jit(solution)/shard_map/all_to_all | solution.py:96
  391.2 56.2 %copy-start.3 = (f32[128]{0:T(128)}, f32[128]{0:T(128)S(1)}, u32[]{:S(2)}) copy-start(f32[128]{0:T(128)S(1)} %compare_select_fusion.2) | copy-start | bytes 1540
  391.9 52.5 %all-to-all-start.3 = ((f32[8,1,16]{2,1,0:T(1,128)}), f32[8,1,16]{2,1,0:T(1,128)S(1)}, u32[]{:S(2)}, u32[]{:S(2)}) async-start(f32[8,1,16]{2,1,0:T(1,128)} %bitcast.29), calls=%async_computation.4 | async-start | bytes 8192 | tf_op jit(solution)/shard_map/all_to_all | solution.py:114
Sparse Core Ops, SparseCore 0:
  23.4 80.6 all-gather.11
  189.2 53.1 reduce-scatter.1
